TPU v7x, 512 devices: a whole 4x4x16 slice. The times are simulated.
512 devices in a mesh: vocab: 64 (over z, x_lo, core), hid: 8 (over x_hi, y).
Axes of the slice: x: 4 (x_hi: 2, x_lo: 2; x = x_hi * 2 + x_lo), y: 4, z: 16, core: 2. Of those that a mesh axis runs over, the one named last changes fastest.
Arguments:
- posterior: bfloat16 [512, 16384], P(None, 'vocab'), may hold values from 1.9e-09 to 1, as said below
- transition: bfloat16 [16384, 16384], P('vocab', 'hid'), may hold values from 1e-07 to 1, as said below
- emission: bfloat16 [16384, 16384], P('hid', 'vocab'), may hold values from 6e-06 to 90, as said below
- advance: bfloat16 [256, 16384], P(None, 'hid'), may hold values from 0.0099487305 to 1
- dfa_state: int32 [512], replicated, may hold values from 0 to 255
- edge_next: int32 [256, 8], replicated, may hold values from 0 to 255
- token_edge: int32 [256, 16384], P(None, 'vocab'), may hold values from 0 to 7
- allowed: int32 [512, 128], P(None, 'vocab'), may hold values from 0 to 1, as said below
Outputs:
- constrained_logprob: float32 [512, 16384], P('hid', 'vocab')
Inputs may be any that keep to these rules, and one draw needn't show every extreme that they name: `allowed`: every request allows at least one block. `posterior`: positive. `transition`: positive. `emission`: positive.
All inputs are finite; a program needn't handle non-finite values.
Results may differ from a plain program's by a relative error of at most 0.0015.
Values may be sent and summed in bfloat16 or wider, within the bound.
A program may use at most 64 MiB of HBM per device.

v0:
```python
import jax
import jax.numpy as jnp
from jax import lax
from jax.sharding import PartitionSpec as P

BLK = 128


def request_scores(prior_rows, dfa_state, edge_next, token_edge, allowed, advance, emission):
    row_count = prior_rows.shape[0]
    successor = jnp.take(edge_next, dfa_state, axis=0)
    look_rows = jnp.take(advance, successor, axis=0)
    weighted = (prior_rows.astype(jnp.float32)[:, None, :] * look_rows.astype(jnp.float32)).astype(
        jnp.bfloat16
    )
    slot_count = successor.shape[1]
    flattened = weighted.reshape(row_count * slot_count, weighted.shape[2])
    candidate = jnp.dot(flattened, emission, preferred_element_type=jnp.float32).reshape(
        row_count, slot_count, emission.shape[1]
    )
    edge_slots = jnp.take(token_edge, dfa_state, axis=0)
    labels = jnp.arange(slot_count, dtype=jnp.int32)
    chosen = jnp.sum(
        jnp.where(edge_slots[:, None, :] == labels[None, :, None], candidate, jnp.float32(0.0)),
        axis=1,
    )
    token_mask = jnp.repeat(allowed, BLK, axis=1)
    return jnp.where(token_mask > 0, chosen, jnp.float32(0.0))


def body(posterior, transition, emission, advance, dfa_state, edge_next, token_edge, allowed):
    prior_own = lax.psum_scatter(
        jnp.dot(posterior, transition, preferred_element_type=jnp.float32),
        "vocab",
        scatter_dimension=0,
        tiled=True,
    ).astype(jnp.bfloat16)
    partials = request_scores(
        lax.all_gather(prior_own, "vocab", axis=0, tiled=True),
        dfa_state,
        edge_next,
        token_edge,
        allowed,
        advance,
        emission,
    )
    scores = lax.psum_scatter(
        partials.astype(jnp.bfloat16), "hid", scatter_dimension=0, tiled=True
    ).astype(jnp.float32)
    local_rows = scores.shape[0]
    first_local = lax.axis_index("hid") * local_rows
    totals = lax.psum(jnp.sum(scores, axis=1), "vocab")
    mask_rows = lax.dynamic_slice_in_dim(allowed, first_local, local_rows, 0)
    token_mask = jnp.repeat(mask_rows, BLK, axis=1) > 0
    safe = jnp.where(token_mask, scores, jnp.float32(1.0))
    return jnp.where(token_mask, jnp.log(safe) - jnp.log(totals)[:, None], jnp.float32(0.0))


def solution(mesh):
    in_specs = (
        P(None, "vocab"),
        P("vocab", "hid"),
        P("hid", "vocab"),
        P(None, "hid"),
        P(),
        P(),
        P(None, "vocab"),
        P(None, "vocab"),
    )
    out_specs = P("hid", "vocab")
    return jax.shard_map(body, mesh=mesh, in_specs=in_specs, out_specs=out_specs, check_vma=False)
```

profile of v0, /device:TPU:1, one launch (start us, length us, event | category | flops | bytes accessed | tf_op | source)
XLA Modules:
  0.0 602.0 jit_solution(13615866778587981965)
XLA Ops:
  6.5 0.0 copy-start
  6.5 0.0 copy-start.1
  6.5 0.0 reduce-scatter.3.cloned.1.call-start
  6.5 4.0 fusion.9
  10.6 0.0 reduce-scatter.3.cloned.1.call-update
  10.6 0.0 all-gather.2.cloned.1.call-start
  10.7 233.8 %reduce-scatter.3.cloned.1.call-done = f32[8,2048]{1,0:T(8,128)} async-done(((f32[512,2048]{1,0:T(8,128)}), f32[8,2048]{1,0:T(8,128)}) %reduce-scatter.3.cloned.1.call-update) | async-done | bytes 65552 | tf_op jit(solution)/shard_map/reduce_scatter | solution.py:32
  244.4 1.5 convert_element_type.22
  245.9 0.0 all-gather.2.cloned.1.call-update
  245.9 0.0 reduce-scatter.5.cloned.1.call-start
  246.0 0.7 broadcast_compare_fusion
  246.7 0.3 copy.18
  247.0 0.8 copy.15
  247.8 0.7 compare_select_fusion.2
  248.5 1.0 gather_fusion.1
  249.5 0.7 compare_and_fusion.1
  250.2 0.2 compare_and_fusion
  250.4 0.1 copy.16
  250.5 0.1 compare_select_fusion
  250.6 0.1 reshape.104
  250.8 0.0 copy-done.1
  250.8 1.6 gather_fusion
  252.4 0.0 copy-done
  252.4 0.0 copy-start.2
  252.4 21.0 %gather_fusion.2 = bf16[4096,2048]{1,0:T(8,128)(2,1)} fusion(bf16[256,2048]{1,0:T(8,128)(2,1)S(1)} %copy-done, s32[4096]{0:T(1024)S(1)} %broadcast_clamp_fusion), kind=kCustom, calls=%fused_computation.2 | custom fusion | bytes 33570816 | tf_op jit(solution)/shard_map/jit(_take)/gather | solution.py:12
  273.4 0.1 broadcast_select_fusion
  273.5 96.2 %all-gather.2.cloned.1.call-done = bf16[512,2048]{1,0:T(8,128)(2,1)} async-done(((bf16[8,2048]{1,0:T(8,128)(2,1)}), bf16[512,2048]{1,0:T(8,128)(2,1)}) %all-gather.2.cloned.1.call-update) | async-done | bytes 2097168 | tf_op jit(solution)/shard_map/all_gather | solution.py:39
  369.8 2.1 convert_element_type.23
  371.9 0.0 copy-done.2
  371.9 33.8 %select_reduce_fusion = bf16[512,256]{1,0:T(8,128)(2,1)S(1)} fusion(s32[512,256]{1,0:T(8,128)S(1)} %broadcast_select_fusion, bf16[512,8,2048]{2,1,0:T(8,128)(2,1)} %bitcast.16, f32[512,2048]{1,0:T(8,128)S(1)} %convert_element_type.23, pred[512,8]{0,1:T(8,128)(4,1)S(1)} %copy.16, bf16[2048,256]{1,0:T(8,128)(2,1)S(1)} %copy-done.2), kind=kOutput, calls=%fused_computation.9 | convolution fusion | flops 4331536384 | bytes 22810624 | tf_op jit(solution)/shard_map/dot_general | solution.py:18
  405.7 0.8 select_convert_fusion
  406.5 0.0 reduce-scatter.5.cloned.1.call-update
  406.5 0.8 dynamic-slice_compare_fusion
  407.3 0.1 copy.14
  407.4 78.4 %reduce-scatter.5.cloned.1.call-done = bf16[64,256]{1,0:T(8,128)(2,1)} async-done(((bf16[512,256]{1,0:T(8,128)(2,1)}), bf16[64,256]{1,0:T(8,128)(2,1)}) %reduce-scatter.5.cloned.1.call-update) | async-done | bytes 32784 | tf_op jit(solution)/shard_map/reduce_scatter | solution.py:47
  485.9 0.9 convert_reduce_fusion
  486.7 107.1 %psum.7 = f32[64]{0:T(128)S(1)} all-reduce(f32[64]{0:T(128)S(1)} %convert_reduce_fusion), channel_id=1, replica_groups=mesh['vocab'=64,'hid'=8] {'vocab'}, use_global_device_ids=true, to_apply=%region_4.5 | all-reduce | flops 64 | bytes 512 | tf_op jit(solution)/shard_map/psum | solution.py:52
  593.9 0.1 broadcast_in_dim.61
  594.0 1.5 fusion.7
  (4 shorter events, 0.1 us)
Async XLA Ops:
  6.5 245.9 %copy-start = (bf16[256,2048]{1,0:T(8,128)(2,1)S(1)}, bf16[256,2048]{1,0:T(8,128)(2,1)}, u32[]{:S(2)}) copy-start(bf16[256,2048]{1,0:T(8,128)(2,1)} %param.11) | copy-start | bytes 3145732
  6.5 244.3 %copy-start.1 = (s32[256,256]{1,0:T(8,128)S(1)}, s32[256,256]{1,0:T(8,128)}, u32[]{:S(2)}) copy-start(s32[256,256]{1,0:T(8,128)} %param.14) | copy-start | bytes 786436
  6.5 237.9 %reduce-scatter.3.cloned.1.call-start = ((), (), s32[]{:S(2)}) async-start(), calls=%async_computation.2 | async-start | bytes 4259840 | tf_op jit(solution)/shard_map/reduce_scatter | solution.py:32
  10.6 359.2 %all-gather.2.cloned.1.call-start = ((), (), s32[]{:S(2)}) async-start(), calls=%async_computation.3 | async-start | bytes 2129920 | tf_op jit(solution)/shard_map/all_gather | solution.py:39
  245.9 240.0 %reduce-scatter.5.cloned.1.call-start = ((), (), s32[]{:S(2)}) async-start(), calls=%async_computation.4 | async-start | bytes 294912 | tf_op jit(solution)/shard_map/reduce_scatter | solution.py:47
  252.4 119.5 %copy-start.2 = (bf16[2048,256]{1,0:T(8,128)(2,1)S(1)}, bf16[2048,256]{1,0:T(8,128)(2,1)}, u32[]{:S(2)}) copy-start(bf16[2048,256]{1,0:T(8,128)(2,1)} %param.10) | copy-start | bytes 3145732
Sparse Core Ops, SparseCore 0:
  10.7 233.6 reduce-scatter.2
  246.8 122.9 all-gather.1
  406.7 79.1 reduce-scatter.4
where the time goes:
time: 603 us; the launch traced here: 602 us
  waiting for transfers between devices  408 us (68%)
  blocking collectives  107 us (18%)
  matrix products  37.9 us (6%)
  local copies, waits for them, and re-layouts  25.2 us (4%)
  between operations  13.2 us (2%)
  other arithmetic  9.95 us (2%)
    reduce_scatter x1, waiting for transfers between devices, body(): lax.psum_scatter(jnp.dot(posterior, transition, preferred_element_type=jn...  234 us
    psum x1, blocking collectives, body(): totals = lax.psum(jnp.sum(scores, axis=1), 'vocab')  107 us
    all_gather x1, waiting for transfers between devices, body(): lax.all_gather(prior_own, 'vocab', axis=0, tiled=True)  96.2 us
    reduce_scatter x1, waiting for transfers between devices, body(): lax.psum_scatter(partials.astype(jnp.bfloat16), 'hid', scatter_dimension=...  78.4 us
    dot_general x1, matrix products, request_scores(): jnp.dot(flattened, emission, preferred_element_type=jnp.float32)  33.8 us
    gather x1, local copies, waits for them, and re-layouts, request_scores(): look_rows = jnp.take(advance, successor, axis=0)  21 us
  transfers between devices with their start and end apart: 3, of which 3 were waited for; matrix products, arithmetic and copies ran while one was open for 5% of the time, Pallas kernels for 0%

commit v1 on v0

v1 whole, which is shorter than its diff:
```python
import jax
import jax.numpy as jnp
from jax import lax
from jax.experimental import pallas as pl
from jax.experimental.pallas import tpu as pltpu
from jax.sharding import PartitionSpec as P

MESH = pl.DeviceIdType.MESH
BF = jnp.bfloat16
F32 = jnp.float32
NZ = 16
CH = 16
HALF = 256
KC = 1024
TK = 256
MW = 384


def remote(src, dst, send, recv, a, b):
    return pltpu.make_async_remote_copy(
        src_ref=src,
        dst_ref=dst,
        send_sem=send,
        recv_sem=recv,
        device_id={"vocab": a, "hid": b},
        device_id_type=MESH,
    )


def kernel(
    post,
    trans,
    em,
    adv,
    dfa,
    edge,
    tedge,
    allow,
    out,
    csend,
    crecv,
    own,
    xsend,
    xrecv,
    zsend,
    zrecv,
    pri,
    em4,
    te_own,
    te4,
    gath,
    wbuf,
    cand,
    hsend,
    hrecv,
    tsend,
    trecv,
    s_c,
    r_c,
    s_x,
    r_x,
    s_z,
    r_z,
    s_g,
    r_g,
    s_e,
    r_e,
    s_t,
    r_t,
    s_h,
    r_h,
    s_s,
    r_s,
    l_e,
):
    a = lax.axis_index("vocab")
    b = lax.axis_index("hid")
    z = a // 4
    q = lax.rem(a, 4)
    xl = q // 2
    core = lax.rem(q, 2)
    ocore = 1 - core
    oxl = 1 - xl
    a_core = 4 * z + 2 * xl + ocore
    a_x = 4 * z + 2 * oxl + core
    a_d = 4 * z + 2 * oxl + ocore

    def zmod(v):
        return lax.rem(v + 2 * NZ, NZ)

    def z_dev(zz):
        return 4 * zz + q

    bar = pltpu.get_barrier_semaphore()

    def sig_group(i, c):
        m = lax.rem(q * 8 + b + i, 32)
        pl.semaphore_signal(
            bar, inc=1, device_id={"vocab": 4 * z + m // 8, "hid": lax.rem(m, 8)}, device_id_type=MESH
        )
        return c

    def sig_z(i, c):
        pl.semaphore_signal(
            bar, inc=1, device_id={"vocab": z_dev(zmod(z + i)), "hid": b}, device_id_type=MESH
        )
        return c

    lax.fori_loop(1, 32, sig_group, 0)
    lax.fori_loop(1, NZ, sig_z, 0)

    def part(row_half, col_half):
        rows = pl.ds(pl.multiple_of(row_half * HALF, HALF), HALF)
        cols = pl.ds(pl.multiple_of(col_half * KC, KC), KC)
        return jnp.dot(post[rows, :], trans[:, cols], preferred_element_type=F32)

    csend[0] = part(ocore, oxl).astype(BF)
    pl.semaphore_wait(bar, 31 + NZ - 1)
    c0 = remote(csend.at[0], crecv.at[0], s_c.at[0], r_c.at[0], a_core, b)
    c0.start()
    csend[1] = part(ocore, xl).astype(BF)
    c1 = remote(csend.at[1], crecv.at[1], s_c.at[1], r_c.at[1], a_core, b)
    c1.start()
    half_rows = pl.ds(pl.multiple_of(xl * KC, KC), KC)
    e_core = remote(em.at[half_rows, :], em4.at[1], s_e.at[0], r_e.at[0], a_core, b)
    e_core.start()
    e_own = pltpu.make_async_copy(em.at[half_rows, :], em4.at[0], l_e)
    e_own.start()
    own[0] = part(core, oxl)
    own[1] = part(core, xl)
    c0.wait_recv()

    def x_step(i, c):
        zc = zmod(z + 8 + i)
        rows = pl.ds(pl.multiple_of(zc * CH, CH), CH)
        xsend[zc] = (own[0, rows, :] + crecv[0, rows, :].astype(F32)).astype(BF)
        remote(xsend.at[zc], xrecv.at[zc], s_x.at[zc], r_x.at[zc], a_x, b).start()
        return c

    def order(i):
        m = 8 - (i + 1) // 2
        return jnp.where(lax.rem(i, 2) == 0, -m, m)

    def x_ord(i, c):
        return x_step(order(i) - 8, c)

    lax.fori_loop(0, NZ, x_ord, 0)
    c1.wait_recv()

    def z_step(i, c):
        zc = zmod(z + order(i))
        d = zmod(order(i))
        rows = pl.ds(pl.multiple_of(zc * CH, CH), CH)
        remote(xsend.at[zc], xrecv.at[zc], s_x.at[zc], r_x.at[zc], a_x, b).wait_recv()
        total = own[1, rows, :] + crecv[1, rows, :].astype(F32) + xrecv[zc].astype(F32)
        zsend[zc] = total.astype(BF)
        remote(zsend.at[zc], zrecv.at[d], s_z.at[d], r_z.at[d], z_dev(zc), b).start()
        return c

    lax.fori_loop(0, NZ - 1, z_step, 0)
    my_rows = pl.ds(pl.multiple_of(z * CH, CH), CH)
    remote(xsend.at[z], xrecv.at[z], s_x.at[z], r_x.at[z], a_x, b).wait_recv()
    own[0, pl.ds(0, CH), :] = own[1, my_rows, :] + crecv[1, my_rows, :].astype(F32) + xrecv[z].astype(F32)

    other_rows = pl.ds(pl.multiple_of(oxl * KC, KC), KC)
    e_x = remote(em.at[other_rows, :], em4.at[2], s_e.at[1], r_e.at[1], a_x, b)
    e_x.start()

    iota_s = lax.broadcasted_iota(jnp.int32, (HALF, HALF), 0)
    iota_l = lax.broadcasted_iota(jnp.int32, (HALF, HALF), 1)
    te_b = tedge[...].astype(F32).astype(BF)
    for which in range(2):
        h = core if which == 0 else ocore
        lanes = pl.ds(pl.multiple_of(h * HALF, HALF), HALF)
        hot_t = jnp.where(iota_s == dfa[:, lanes], 1.0, 0.0).astype(F32)
        hot = jnp.transpose(hot_t).astype(BF)
        te_h = jnp.dot(hot, te_b, preferred_element_type=F32)
        al = allow[:, lanes].astype(F32)
        al_pad = jnp.concatenate([al, jnp.zeros((126, HALF), F32)], axis=0)
        al_t = jnp.transpose(al_pad)
        ok = jnp.where(iota_l < 128, al_t[:, 0:1], al_t[:, 1:2])
        te_own[h] = jnp.where(ok > 0.0, te_h, 8.0).astype(BF)
        if which == 0:
            suc_t = jnp.dot(edge[...].astype(F32).astype(BF), hot_t.astype(BF), preferred_element_type=F32)
            suc_pad = jnp.concatenate([suc_t, jnp.zeros((120, HALF), F32)], axis=0)
            suc = jnp.transpose(suc_pad).astype(jnp.int32)
    te4[0] = te_own[core]
    t_core = remote(te_own.at[ocore], te4.at[1], s_t.at[0], r_t.at[0], a_core, b)
    t_x = remote(te_own.at[core], te4.at[2], s_t.at[1], r_t.at[1], a_x, b)
    t_d = remote(te_own.at[ocore], te4.at[3], s_t.at[2], r_t.at[2], a_d, b)
    t_core.start()
    t_x.start()
    t_d.start()
    half_cols = pl.ds(pl.multiple_of(xl * KC, KC), KC)
    for k in range(8):
        hot2 = jnp.where(iota_l == suc[:, k : k + 1], 1.0, 0.0).astype(F32).astype(BF)
        g = jnp.dot(hot2, adv[:, half_cols], preferred_element_type=F32).astype(BF)
        gath[k] = g.reshape(NZ, CH, KC)

    def z_add(i, c):
        d = zmod(order(i))
        remote(zsend.at[0], zrecv.at[d], s_z.at[d], r_z.at[d], z_dev(z), b).wait_recv()
        own[0, pl.ds(0, CH), :] += zrecv[d].astype(F32)
        return c

    lax.fori_loop(0, NZ - 1, z_add, 0)
    pri[z] = own[0, pl.ds(0, CH), :].astype(BF)

    def ag_step(i, c):
        d = zmod(order(i))
        remote(pri.at[z], pri.at[z], s_g.at[d], r_g.at[d], z_dev(zmod(z + d)), b).start()
        return c

    lax.fori_loop(0, NZ - 1, ag_step, 0)

    e_x.wait_recv()
    e_f = remote(em4.at[2], em4.at[3], s_e.at[2], r_e.at[2], a_core, b)
    e_f.start()
    e_own.wait()
    e_core.wait_recv()
    t_core.wait_recv()
    t_x.wait_recv()
    t_d.wait_recv()
    e_f.wait_recv()

    lane = lax.broadcasted_iota(jnp.int32, (2 * CH, 128), 1)
    src = xl * 8 + b

    def hid_copy(zc, j):
        qa = [q, 2 * xl + ocore, 2 * oxl + core, 2 * oxl + ocore][j]
        dst = hrecv.at[src, pl.ds(pl.multiple_of(lax.rem(zc, 4) * CH, CH), CH), :]
        return remote(hsend.at[zc, j], dst, s_h.at[zc, j], r_h.at[src], 4 * z + qa, 4 * core + zc // 4)

    def hid_local(zc):
        dst = hrecv.at[src, pl.ds(pl.multiple_of(lax.rem(zc, 4) * CH, CH), CH), :]
        return pltpu.make_async_copy(hsend.at[zc, 0], dst, r_h.at[src])

    def score(t, c):
        zc0 = zmod(z - t)
        zc1 = zmod(z + t + 1)

        @pl.when(t > 0)
        def _():
            remote(pri.at[z], pri.at[zc0], s_g.at[t], r_g.at[t], z_dev(z), b).wait_recv()

        d1 = NZ - 1 - t
        remote(pri.at[z], pri.at[zc1], s_g.at[d1], r_g.at[d1], z_dev(z), b).wait_recv()
        x0 = pri[zc0]
        x1 = pri[zc1]
        for k in range(8):
            wbuf[pl.ds(k * 2 * CH, CH), :] = gath[k, zc0] * x0
            wbuf[pl.ds(k * 2 * CH + CH, CH), :] = gath[k, zc1] * x1
        tot = jnp.zeros((2 * CH, 1), F32)
        for j in range(4):
            cand[...] = jnp.dot(wbuf[...], em4[j], preferred_element_type=F32)
            te = jnp.concatenate(
                [
                    te4[j, pl.ds(pl.multiple_of(zc0 * CH, CH), CH), :],
                    te4[j, pl.ds(pl.multiple_of(zc1 * CH, CH), CH), :],
                ],
                axis=0,
            ).astype(F32)
            chosen = jnp.zeros((2 * CH, TK), F32)
            for k in range(8):
                chosen = jnp.where(te == float(k), cand[pl.ds(k * 2 * CH, 2 * CH), :], chosen)
            tot = tot + jnp.sum(chosen, axis=1, keepdims=True)
            picked = chosen.astype(BF)
            hsend[zc0, j, :, pl.ds(0, TK)] = picked[:CH]
            hsend[zc1, j, :, pl.ds(0, TK)] = picked[CH:]
        hi = tot.astype(BF).astype(F32)
        lo = tot - hi
        tile = jnp.where(lane == 0, hi, jnp.where(lane == 1, lo, 0.0)).astype(BF)
        for j in range(4):
            hsend[zc0, j, :, pl.ds(TK, 128)] = tile[:CH]
            hsend[zc1, j, :, pl.ds(TK, 128)] = tile[CH:]
        for zc in (zc0, zc1):
            for j in (3, 2, 1):
                hid_copy(zc, j).start()
            mine = 4 * core + zc // 4 == b

            @pl.when(mine)
            def _():
                hid_local(zc).start()

            @pl.when(jnp.logical_not(mine))
            def _():
                hid_copy(zc, 0).start()

        return c

    lax.fori_loop(0, NZ // 2, score, 0)

    def h_wait(i, c):
        remote(hrecv.at[i], hrecv.at[i], s_h.at[0, 0], r_h.at[i], a_core, b).wait_recv()
        return c

    lax.fori_loop(0, 16, h_wait, 0)
    acc = jnp.zeros((64, MW), F32)
    for i in range(16):
        acc = acc + hrecv[i].astype(F32)
    scores = acc[:, :TK]
    quad_tot = jnp.sum(acc[:, TK:], axis=1, keepdims=True)
    spread = jnp.concatenate([jnp.broadcast_to(quad_tot, (64, 128)), jnp.zeros((64, 128), F32)], axis=0)
    tsend[...] = jnp.transpose(spread)[0:1]

    def t_step(i, c):
        d = zmod(order(i))
        remote(tsend, trecv.at[d], s_s.at[d], r_s.at[d], z_dev(zmod(z + d)), b).start()
        return c

    lax.fori_loop(0, NZ - 1, t_step, 0)
    mask = te_own[b // 4, pl.ds(pl.multiple_of(lax.rem(b, 4) * 64, 64), 64), :].astype(F32) < 7.5
    logs = jnp.log(jnp.where(mask, scores, 1.0))
    trecv[0] = tsend[...]

    def t_wait(i, c):
        d = zmod(order(i))
        remote(tsend, trecv.at[d], s_s.at[d], r_s.at[d], z_dev(z), b).wait_recv()
        return c

    lax.fori_loop(0, NZ - 1, t_wait, 0)
    full = jnp.zeros((1, 128), F32)
    for d in range(NZ):
        full = full + trecv[d]
    column = jnp.transpose(jnp.broadcast_to(full, (128, 128)))[:64, 0:1]
    out[...] = jnp.where(mask, logs - jnp.log(column), 0.0)

    c0.wait_send()
    c1.wait_send()
    for cp in (e_core, e_x, e_f, t_core, t_x, t_d):
        cp.wait_send()

    def drain(i, c):
        remote(xsend.at[i], xrecv.at[i], s_x.at[i], r_x.at[i], a_x, b).wait_send()
        for j in (1, 2, 3):
            hid_copy(i, j).wait_send()

        @pl.when(4 * core + i // 4 != b)
        def _():
            hid_copy(i, 0).wait_send()

        @pl.when(i > 0)
        def _():
            remote(zsend.at[0], zrecv.at[i], s_z.at[i], r_z.at[i], z_dev(z), b).wait_send()
            remote(pri.at[z], pri.at[z], s_g.at[i], r_g.at[i], z_dev(z), b).wait_send()
            remote(tsend, trecv.at[i], s_s.at[i], r_s.at[i], z_dev(z), b).wait_send()

        return c

    lax.fori_loop(0, NZ, drain, 0)


def body(posterior, transition, emission, advance, dfa_state, edge_next, token_edge, allowed):
    vm = pl.BlockSpec(memory_space=pltpu.VMEM)
    dma = pltpu.SemaphoreType.DMA
    return pl.pallas_call(
        kernel,
        out_shape=jax.ShapeDtypeStruct((64, TK), F32),
        in_specs=[vm] * 8,
        out_specs=vm,
        scratch_shapes=[
            pltpu.VMEM((2, HALF, KC), BF),
            pltpu.VMEM((2, HALF, KC), BF),
            pltpu.VMEM((2, HALF, KC), F32),
            pltpu.VMEM((NZ, CH, KC), BF),
            pltpu.VMEM((NZ, CH, KC), BF),
            pltpu.VMEM((NZ, CH, KC), BF),
            pltpu.VMEM((NZ, CH, KC), BF),
            pltpu.VMEM((NZ, CH, KC), BF),
            pltpu.VMEM((4, KC, TK), BF),
            pltpu.VMEM((2, HALF, TK), BF),
            pltpu.VMEM((4, HALF, TK), BF),
            pltpu.VMEM((8, NZ, CH, KC), BF),
            pltpu.VMEM((HALF, KC), BF),
            pltpu.VMEM((HALF, TK), F32),
            pltpu.VMEM((NZ, 4, CH, MW), BF),
            pltpu.VMEM((16, 64, MW), BF),
            pltpu.VMEM((1, 128), F32),
            pltpu.VMEM((NZ, 1, 128), F32),
            dma((2,)),
            dma((2,)),
            dma((NZ,)),
            dma((NZ,)),
            dma((NZ,)),
            dma((NZ,)),
            dma((NZ,)),
            dma((NZ,)),
            dma((3,)),
            dma((3,)),
            dma((3,)),
            dma((3,)),
            dma((NZ, 4)),
            dma((16,)),
            dma((NZ,)),
            dma((NZ,)),
            dma,
        ],
        compiler_params=pltpu.CompilerParams(
            collective_id=0, has_side_effects=True, vmem_limit_bytes=48 * 1024 * 1024
        ),
        name="constrained",
    )(
        posterior,
        transition,
        emission,
        advance,
        dfa_state.reshape(1, 512),
        edge_next.T,
        token_edge,
        allowed.T,
    )


def solution(mesh):
    in_specs = (
        P(None, "vocab"),
        P("vocab", "hid"),
        P("hid", "vocab"),
        P(None, "hid"),
        P(),
        P(),
        P(None, "vocab"),
        P(None, "vocab"),
    )
    out_specs = P("hid", "vocab")
    return jax.shard_map(body, mesh=mesh, in_specs=in_specs, out_specs=out_specs, check_vma=False)
```

time: 603 us -> 106 us (0.18)
  waiting for transfers between devices: 408 us -> 0 us
  blocking collectives: 107 us -> 0 us
  Pallas kernels: 0 us -> 97.5 us
  matrix products: 37.9 us -> 0 us
  local copies, waits for them, and re-layouts: 25.2 us -> 8.27 us
  between operations: 13.2 us -> 0.02 us
  other arithmetic: 9.95 us -> 0 us
    reduce_scatter x2 -> x0, waiting for transfers between devices: 312 us -> none  [the longest x1 234 us: body(): lax.psum_scatter(jnp.dot(posterior, transition, preferred_element_type=jn...]
    psum x1 -> x0, blocking collectives: 107 us -> none  [body(): totals = lax.psum(jnp.sum(scores, axis=1), 'vocab')]
    pallas_call x0 -> x1, Pallas kernels: none -> 97.5 us  [body(): pl.pallas_call(kernel, out_shape=jax.ShapeDtypeStruct((64, TK), F32), in_...]
    all_gather x1 -> x0, waiting for transfers between devices: 96.2 us -> none  [body(): lax.all_gather(prior_own, 'vocab', axis=0, tiled=True)]
    dot_general x2 -> x0, matrix products: 37.9 us -> none  [the longest x1 33.8 us: request_scores(): jnp.dot(flattened, emission, preferred_element_type=jnp.float32)]
    gather x3 -> x0, local copies, waits for them, and re-layouts: 23.6 us -> none  [the longest x1 21 us: request_scores(): look_rows = jnp.take(advance, successor, axis=0)]
    unnamed x7 -> x17, local copies, waits for them, and re-layouts: 0.84 us -> 8.27 us
  transfers between devices with their start and end apart: 3 -> 0, of which waited for: 3 -> 0; matrix products, arithmetic and copies ran while one was open for 5% -> 0% of each run, Pallas kernels for 0% -> 0%
where the time goes in v1:
time: 106 us
  Pallas kernels  97.5 us (92%)
  local copies, waits for them, and re-layouts  8.27 us (8%)
    pallas_call x1, Pallas kernels, body(): pl.pallas_call(kernel, out_shape=jax.ShapeDtypeStruct((64, TK), F32), in_...  97.5 us
    unnamed x17, local copies, waits for them, and re-layouts  8.27 us

profile of v1, /device:TPU:1, one launch (start us, length us, event | category | flops | bytes accessed | tf_op | source)
XLA Modules:
  0.0 105.8 jit_solution(5855183246636331080)
XLA Ops:
  0.0 0.0 copy-start.6
  0.0 0.7 copy-done.6
  0.7 0.0 copy-start
  0.7 1.2 %copy-done = bf16[256,2048]{1,0:T(8,128)(2,1)S(1)} copy-done((bf16[256,2048]{1,0:T(8,128)(2,1)S(1)}, bf16[256,2048]{1,0:T(8,128)(2,1)}, u32[]{:S(2)}) %copy-start) | copy-done | bytes 1048600
  1.9 0.0 copy-start.1
  1.9 1.2 %copy-done.1 = bf16[2048,256]{1,0:T(8,128)(2,1)S(1)} copy-done((bf16[2048,256]{1,0:T(8,128)(2,1)S(1)}, bf16[2048,256]{1,0:T(8,128)(2,1)}, u32[]{:S(2)}) %copy-start.1) | copy-done | bytes 1048600
  3.1 0.0 copy-start.2
  3.1 1.2 %copy-done.2 = bf16[256,2048]{1,0:T(8,128)(2,1)S(1)} copy-done((bf16[256,2048]{1,0:T(8,128)(2,1)S(1)}, bf16[256,2048]{1,0:T(8,128)(2,1)}, u32[]{:S(2)}) %copy-start.2) | copy-done | bytes 1048600
  4.4 0.0 copy-start.3
  4.4 0.9 copy-done.3
  5.3 0.0 copy-start.4
  5.3 0.9 copy-done.4
  6.3 0.0 copy-start.5
  6.3 0.7 copy-done.5
  7.0 0.0 copy-start.7
  7.0 0.7 copy-done.7
  7.6 97.5 %constrained.1 = f32[64,256]{1,0:T(8,128)S(1)} custom-call(bf16[512,256]{1,0:T(8,128)(2,1)S(1)} %copy-done.3, bf16[256,2048]{1,0:T(8,128)(2,1)S(1)} %copy-done, bf16[2048,256]{1,0:T(8,128)(2,1)S(1)} %copy-done.1, bf16[256,2048]{1,0:T(8,128)(2,1)S(1)} %copy-done.2, s32[1,512]{1,0:T(1,128)S(1)} %bitcast.5, s32[8,256]{1,0:T(8,128)S(1)} %bitcast.3, ...), custom_call_target="tpu_custom_call" | custom-call | tf_op jit(solution)/shard_map/constrained/pallas_call | solution.py:356
  105.2 0.6 copy.10
Async XLA Ops:
  0.0 0.7 copy-start.6
  0.7 1.2 %copy-start = (bf16[256,2048]{1,0:T(8,128)(2,1)S(1)}, bf16[256,2048]{1,0:T(8,128)(2,1)}, u32[]{:S(2)}) copy-start(bf16[256,2048]{1,0:T(8,128)(2,1)} %trans.1) | copy-start | bytes 3145732
  1.9 1.2 %copy-start.1 = (bf16[2048,256]{1,0:T(8,128)(2,1)S(1)}, bf16[2048,256]{1,0:T(8,128)(2,1)}, u32[]{:S(2)}) copy-start(bf16[2048,256]{1,0:T(8,128)(2,1)} %em.1) | copy-start | bytes 3145732
  3.1 1.2 %copy-start.2 = (bf16[256,2048]{1,0:T(8,128)(2,1)S(1)}, bf16[256,2048]{1,0:T(8,128)(2,1)}, u32[]{:S(2)}) copy-start(bf16[256,2048]{1,0:T(8,128)(2,1)} %adv.1) | copy-start | bytes 3145732
  4.4 0.9 copy-start.3
  5.3 0.9 copy-start.4
  6.3 0.7 copy-start.5
  7.0 0.7 copy-start.7

commit v2 on v1

v2 whole, which is shorter than its diff:
```python
import jax
import jax.numpy as jnp
from jax import lax
from jax.experimental import pallas as pl
from jax.experimental.pallas import tpu as pltpu
from jax.sharding import PartitionSpec as P

MESH = pl.DeviceIdType.MESH
BF = jnp.bfloat16
F32 = jnp.float32
NZ = 16
CH = 16
HALF = 256
KC = 1024
TK = 256
MW = 384
TARGET = {
    -3: 2, -4: 1, -6: -1, -7: -2, 8: -3, 3: -2, 4: -1, 6: 1, 7: 2,
    1: 1, -1: -1, 2: 2, -2: -2, 5: 5, -5: -5,
}
FIRST = (8, -3, 3, -7, 7, -4, 4, -6, 6)
X_ORDER = FIRST + (-5, 5, -2, 2, -1, 1, 0)
BARRIER_STEPS = (5, -5, 3, -3, 2, -2, 1, -1)


def remote(src, dst, send, recv, a, b):
    return pltpu.make_async_remote_copy(
        src_ref=src,
        dst_ref=dst,
        send_sem=send,
        recv_sem=recv,
        device_id={"vocab": a, "hid": b},
        device_id_type=MESH,
    )


def kernel(
    post_h,
    trans_h,
    em_h,
    adv_h,
    dfa_h,
    edge_h,
    tedge_h,
    allow_h,
    out,
    post,
    trans,
    adv,
    dfa,
    edge,
    tedge,
    allow,
    csend,
    crecv,
    own,
    xsend,
    xrecv,
    zsend,
    zrecv,
    agg,
    pri,
    em4,
    tab4,
    te4,
    gath,
    wbuf,
    cand,
    hsend,
    hrecv,
    tsend,
    trecv,
    allowed_rows,
    l_in,
    s_c,
    r_c,
    s_x,
    r_x,
    s_z,
    r_z,
    s_g,
    r_g,
    s_e,
    r_e,
    s_t,
    r_t,
    s_h,
    r_h,
    s_s,
    r_s,
):
    a = lax.axis_index("vocab")
    b = lax.axis_index("hid")
    z = a // 4
    q = lax.rem(a, 4)
    xl = q // 2
    core = lax.rem(q, 2)
    ocore = 1 - core
    oxl = 1 - xl
    a_core = 4 * z + 2 * xl + ocore
    a_x = 4 * z + 2 * oxl + core

    half_rows = pl.ds(pl.multiple_of(xl * KC, KC), KC)
    other_rows = pl.ds(pl.multiple_of(oxl * KC, KC), KC)
    loads = [
        pltpu.make_async_copy(post_h, post, l_in.at[0]),
        pltpu.make_async_copy(trans_h, trans, l_in.at[1]),
        pltpu.make_async_copy(tedge_h, tedge, l_in.at[2]),
        pltpu.make_async_copy(allow_h, allow, l_in.at[3]),
        pltpu.make_async_copy(dfa_h, dfa, l_in.at[4]),
        pltpu.make_async_copy(edge_h, edge, l_in.at[5]),
        pltpu.make_async_copy(adv_h.at[:, half_rows], adv, l_in.at[6]),
        pltpu.make_async_copy(em_h.at[half_rows, :], em4.at[0], l_in.at[7]),
    ]
    for cp in loads:
        cp.start()

    def zmod(v):
        return lax.rem(v + 2 * NZ, NZ)

    def z_dev(step):
        return 4 * zmod(z + step) + q

    bar = pltpu.get_barrier_semaphore()

    def sig_group(i, c):
        m = lax.rem(q * 8 + b + i, 32)
        pl.semaphore_signal(
            bar, inc=1, device_id={"vocab": 4 * z + m // 8, "hid": lax.rem(m, 8)}, device_id_type=MESH
        )
        return c

    for step in BARRIER_STEPS:
        pl.semaphore_signal(bar, inc=1, device_id={"vocab": z_dev(step), "hid": b}, device_id_type=MESH)
    lax.fori_loop(1, 32, sig_group, 0)

    def part(row_half, col_half):
        rows = pl.ds(pl.multiple_of(row_half * HALF, HALF), HALF)
        cols = pl.ds(pl.multiple_of(col_half * KC, KC), KC)
        return jnp.dot(post[rows, :], trans[:, cols], preferred_element_type=F32)

    loads[0].wait()
    loads[1].wait()
    csend[0] = part(ocore, oxl).astype(BF)
    pl.semaphore_wait(bar, 31 + len(BARRIER_STEPS))
    c0 = remote(csend.at[0], crecv.at[0], s_c.at[0], r_c.at[0], a_core, b)
    c0.start()
    csend[1] = part(ocore, xl).astype(BF)
    c1 = remote(csend.at[1], crecv.at[1], s_c.at[1], r_c.at[1], a_core, b)
    c1.start()

    loads[2].wait()
    loads[3].wait()
    tab4[0, pl.ds(0, HALF), :] = tedge[...].astype(F32).astype(BF)
    al = allow[...].astype(F32)
    al_rows = jnp.concatenate([al[:, :HALF], al[:, HALF:], jnp.zeros((12, HALF), F32)], axis=0)
    tab4[0, pl.ds(HALF, 16), :] = al_rows.astype(BF)
    t_core = remote(tab4.at[0], tab4.at[1], s_t.at[0], r_t.at[0], a_core, b)
    t_x = remote(tab4.at[0], tab4.at[2], s_t.at[1], r_t.at[1], a_x, b)
    t_core.start()
    t_x.start()

    own[0] = part(core, oxl)
    own[1] = part(core, xl)
    c0.wait_recv()

    def x_copy(zc):
        return remote(xsend.at[zc], xrecv.at[zc], s_x.at[zc], r_x.at[zc], a_x, b)

    for o in X_ORDER:
        zc = zmod(z + o)
        rows = pl.ds(pl.multiple_of(zc * CH, CH), CH)
        xsend[zc] = (own[0, rows, :] + crecv[0, rows, :].astype(F32)).astype(BF)
        x_copy(zc).start()
    e_core = remote(em_h.at[half_rows, :], em4.at[1], s_e.at[0], r_e.at[0], a_core, b)
    e_core.start()
    c1.wait_recv()

    def reduced(o):
        zc = zmod(z + o)
        rows = pl.ds(pl.multiple_of(zc * CH, CH), CH)
        x_copy(zc).wait_recv()
        return own[1, rows, :] + crecv[1, rows, :].astype(F32) + xrecv[zc].astype(F32)

    def z_copy(o):
        i = o % NZ
        return remote(zsend.at[i], zrecv.at[i], s_z.at[i], r_z.at[i], z_dev(TARGET[o]), b)

    def z_send(o, value):
        zsend[o % NZ] = value.astype(BF)
        z_copy(o).start()

    def z_take(o):
        z_copy(o).wait_recv()
        return zrecv[o % NZ].astype(F32)

    for o in FIRST:
        z_send(o, reduced(o))
    agg[0] = reduced(-5)
    agg[1] = reduced(5)
    for o in (-2, 2):
        z_send(o, reduced(o))
    total = agg[0]
    for o in (-3, -4, -6, -7, 8):
        total = total + z_take(o)
    z_send(-5, total)
    total = agg[1]
    for o in (3, 4, 6, 7):
        total = total + z_take(o)
    z_send(5, total)
    for o in (-1, 1):
        z_send(o, reduced(o))
    agg[0] = reduced(0)

    e_x = remote(em_h.at[other_rows, :], em4.at[2], s_e.at[1], r_e.at[1], a_x, b)
    e_x.start()
    t_x.wait_recv()
    t_f = remote(tab4.at[2], tab4.at[3], s_t.at[2], r_t.at[2], a_core, b)
    t_f.start()

    for i in (4, 5, 6):
        loads[i].wait()
    iota_s = lax.broadcasted_iota(jnp.int32, (HALF, HALF), 0)
    iota_l = lax.broadcasted_iota(jnp.int32, (HALF, HALF), 1)
    lanes = pl.ds(pl.multiple_of(core * HALF, HALF), HALF)
    hot_t = jnp.where(iota_s == dfa[:, lanes], 1.0, 0.0).astype(F32)
    suc_t = jnp.dot(edge[...].astype(F32).astype(BF), hot_t.astype(BF), preferred_element_type=F32)
    suc = jnp.transpose(jnp.concatenate([suc_t, jnp.zeros((120, HALF), F32)], axis=0)).astype(jnp.int32)
    for k in range(8):
        hot2 = jnp.where(iota_l == suc[:, k : k + 1], 1.0, 0.0).astype(F32).astype(BF)
        g = jnp.dot(hot2, adv[...], preferred_element_type=F32).astype(BF)
        gath[k] = g.reshape(NZ, CH, KC)

    total = agg[0]
    for o in (-1, 1, -2, 2, -5, 5):
        total = total + z_take(o)
    pri[z] = total.astype(BF)

    def g_copy(chunk, step, o):
        zc = zmod(z + chunk)
        i = o % NZ
        return remote(pri.at[zc], pri.at[zc], s_g.at[i], r_g.at[i], z_dev(step), b)

    for step in (5, -5, 1, -1, 2, -2):
        g_copy(0, step, -step).start()

    hot = jnp.transpose(hot_t).astype(BF)
    t_core.wait_recv()
    t_f.wait_recv()
    for j in range(4):
        te = jnp.dot(hot, tab4[j, pl.ds(0, HALF), :], preferred_element_type=F32)
        al = tab4[j, pl.ds(HALF, 16), :].astype(F32)
        al = jnp.where(core == 0, al[0:2], al[2:4])
        al_t = jnp.transpose(jnp.concatenate([al, jnp.zeros((126, HALF), F32)], axis=0))
        ok = jnp.where(iota_l < 128, al_t[:, 0:1], al_t[:, 1:2])
        te4[j] = jnp.where(ok > 0.0, te, 8.0).astype(BF)

    lane = lax.broadcasted_iota(jnp.int32, (2 * CH, 128), 1)
    src = xl * 8 + b

    def hid_copy(zc, j):
        qa = [q, 2 * xl + ocore, 2 * oxl + core, 2 * oxl + ocore][j]
        dst = hrecv.at[src, pl.ds(pl.multiple_of(lax.rem(zc, 4) * CH, CH), CH), :]
        return remote(hsend.at[zc, j], dst, s_h.at[zc, j], r_h.at[src], 4 * z + qa, 4 * core + zc // 4)

    def hid_local(zc):
        dst = hrecv.at[src, pl.ds(pl.multiple_of(lax.rem(zc, 4) * CH, CH), CH), :]
        return pltpu.make_async_copy(hsend.at[zc, 0], dst, r_h.at[src])

    def pri_wait(o):
        i = zmod(o)
        zc = zmod(z + o)
        remote(pri.at[z], pri.at[zc], s_g.at[i], r_g.at[i], z_dev(1), b).wait_recv()

    def score(t, c):
        m = jnp.where(t < 2, t + 1, jnp.where(t == 2, 5, jnp.where(t == 3, 4, jnp.where(t == 4, 3, t + 1))))
        o0 = jnp.where(t == 7, 0, -m)
        zc0 = zmod(z + o0)
        zc1 = zmod(z + m)

        @pl.when(jnp.logical_and(t != 7, t != 2))
        def _():
            pri_wait(o0)

        @pl.when(t != 2)
        def _():
            pri_wait(m)

        x0 = pri[zc0]
        x1 = pri[zc1]
        for k in range(8):
            wbuf[pl.ds(k * 2 * CH, CH), :] = gath[k, zc0] * x0
            wbuf[pl.ds(k * 2 * CH + CH, CH), :] = gath[k, zc1] * x1
        for j in range(4):
            cand[j] = jnp.dot(wbuf[...], em4[j], preferred_element_type=F32)
        tot = jnp.zeros((2 * CH, 1), F32)
        for j in range(4):
            te = jnp.concatenate(
                [
                    te4[j, pl.ds(pl.multiple_of(zc0 * CH, CH), CH), :],
                    te4[j, pl.ds(pl.multiple_of(zc1 * CH, CH), CH), :],
                ],
                axis=0,
            ).astype(F32)
            chosen = jnp.zeros((2 * CH, TK), F32)
            for k in range(8):
                chosen = jnp.where(te == float(k), cand[j, pl.ds(k * 2 * CH, 2 * CH), :], chosen)
            tot = tot + jnp.sum(chosen, axis=1, keepdims=True)
            picked = chosen.astype(BF)
            hsend[zc0, j, :, pl.ds(0, TK)] = picked[:CH]
            hsend[zc1, j, :, pl.ds(0, TK)] = picked[CH:]
        hi = tot.astype(BF).astype(F32)
        lo = tot - hi
        tile = jnp.where(lane == 0, hi, jnp.where(lane == 1, lo, 0.0)).astype(BF)
        for j in range(4):
            hsend[zc0, j, :, pl.ds(TK, 128)] = tile[:CH]
            hsend[zc1, j, :, pl.ds(TK, 128)] = tile[CH:]
        for zc in (zc0, zc1):
            for j in (3, 2, 1):
                hid_copy(zc, j).start()
            mine = 4 * core + zc // 4 == b

            @pl.when(mine)
            def _():
                hid_local(zc).start()

            @pl.when(jnp.logical_not(mine))
            def _():
                hid_copy(zc, 0).start()

        @pl.when(t == 1)
        def _():
            pri_wait(-5)
            for step in (3, -2, 2, -1, 1):
                g_copy(-5, step, -5 - step).start()
            pri_wait(5)
            for step in (2, -2, 1, -1):
                g_copy(5, step, 5 - step).start()

        return c

    loads[7].wait()
    e_core.wait_recv()
    e_x.wait_recv()
    e_f = remote(em4.at[2], em4.at[3], s_e.at[2], r_e.at[2], a_core, b)
    e_f.start()
    e_f.wait_recv()
    lax.fori_loop(0, NZ // 2, score, 0)

    def h_wait(i, c):
        remote(hrecv.at[i], hrecv.at[i], s_h.at[0, 0], r_h.at[i], a_core, b).wait_recv()
        return c

    lax.fori_loop(0, 16, h_wait, 0)
    acc = jnp.zeros((64, MW), F32)
    for i in range(16):
        acc = acc + hrecv[i].astype(F32)
    scores = acc[:, :TK]
    quad_tot = jnp.sum(acc[:, TK:], axis=1, keepdims=True)
    spread = jnp.concatenate([jnp.broadcast_to(quad_tot, (64, 128)), jnp.zeros((64, 128), F32)], axis=0)
    tsend[...] = jnp.transpose(spread)[0:1]

    def t_copy(i):
        d = zmod(i)
        return remote(tsend, trecv.at[d], s_s.at[d], r_s.at[d], z_dev(i), b)

    def t_step(i, c):
        t_copy(lax.rem(i + 7, 15) + 1).start()
        return c

    lax.fori_loop(0, NZ - 1, t_step, 0)
    al = tab4[0, pl.ds(HALF, 16), :].astype(F32)
    al = jnp.where(b < 4, al[0:2], al[2:4])
    al_t = jnp.transpose(jnp.concatenate([al, jnp.zeros((126, HALF), F32)], axis=0))
    allowed_rows[...] = al_t
    al_t = allowed_rows[pl.ds(pl.multiple_of(lax.rem(b, 4) * 64, 64), 64), :]
    lane_v = lax.broadcasted_iota(jnp.int32, (64, TK), 1)
    mask = jnp.where(lane_v < 128, al_t[:, 0:1], al_t[:, 1:2]) > 0.0
    logs = jnp.log(jnp.where(mask, scores, 1.0))
    trecv[0] = tsend[...]

    def t_wait(i, c):
        t_copy(i).wait_recv()
        return c

    lax.fori_loop(1, NZ, t_wait, 0)
    full = jnp.zeros((1, 128), F32)
    for d in range(NZ):
        full = full + trecv[d]
    column = jnp.transpose(jnp.broadcast_to(full, (128, 128)))[:64, 0:1]
    out[...] = jnp.where(mask, logs - jnp.log(column), 0.0)

    for cp in (c0, c1, e_core, e_x, e_f, t_core, t_x, t_f):
        cp.wait_send()

    def drain(i, c):
        x_copy(i).wait_send()
        for j in (1, 2, 3):
            hid_copy(i, j).wait_send()

        @pl.when(4 * core + i // 4 != b)
        def _():
            hid_copy(i, 0).wait_send()

        @pl.when(i > 0)
        def _():
            remote(zsend.at[i], zrecv.at[i], s_z.at[i], r_z.at[i], z_dev(1), b).wait_send()
            remote(pri.at[z], pri.at[z], s_g.at[i], r_g.at[i], z_dev(1), b).wait_send()
            t_copy(i).wait_send()

        return c

    lax.fori_loop(0, NZ, drain, 0)


def body(posterior, transition, emission, advance, dfa_state, edge_next, token_edge, allowed):
    vm = pl.BlockSpec(memory_space=pltpu.VMEM)
    dma = pltpu.SemaphoreType.DMA
    return pl.pallas_call(
        kernel,
        out_shape=jax.ShapeDtypeStruct((64, TK), F32),
        in_specs=[pl.BlockSpec(memory_space=pltpu.HBM)] * 8,
        out_specs=vm,
        scratch_shapes=[
            pltpu.VMEM((512, 256), BF),
            pltpu.VMEM((256, 2 * KC), BF),
            pltpu.VMEM((256, KC), BF),
            pltpu.VMEM((1, 512), jnp.int32),
            pltpu.VMEM((8, 256), jnp.int32),
            pltpu.VMEM((256, TK), jnp.int32),
            pltpu.VMEM((2, 512), jnp.int32),
            pltpu.VMEM((2, HALF, KC), BF),
            pltpu.VMEM((2, HALF, KC), BF),
            pltpu.VMEM((2, HALF, KC), F32),
            pltpu.VMEM((NZ, CH, KC), BF),
            pltpu.VMEM((NZ, CH, KC), BF),
            pltpu.VMEM((NZ, CH, KC), BF),
            pltpu.VMEM((NZ, CH, KC), BF),
            pltpu.VMEM((2, CH, KC), F32),
            pltpu.VMEM((NZ, CH, KC), BF),
            pltpu.VMEM((4, KC, TK), BF),
            pltpu.VMEM((4, HALF + 16, TK), BF),
            pltpu.VMEM((4, HALF, TK), BF),
            pltpu.VMEM((8, NZ, CH, KC), BF),
            pltpu.VMEM((HALF, KC), BF),
            pltpu.VMEM((4, HALF, TK), F32),
            pltpu.VMEM((NZ, 4, CH, MW), BF),
            pltpu.VMEM((16, 64, MW), BF),
            pltpu.VMEM((1, 128), F32),
            pltpu.VMEM((NZ, 1, 128), F32),
            pltpu.VMEM((HALF, 128), F32),
            dma((8,)),
            dma((2,)),
            dma((2,)),
            dma((NZ,)),
            dma((NZ,)),
            dma((NZ,)),
            dma((NZ,)),
            dma((NZ,)),
            dma((NZ,)),
            dma((3,)),
            dma((3,)),
            dma((3,)),
            dma((3,)),
            dma((NZ, 4)),
            dma((16,)),
            dma((NZ,)),
            dma((NZ,)),
        ],
        compiler_params=pltpu.CompilerParams(
            collective_id=0, has_side_effects=True, vmem_limit_bytes=62 * 1024 * 1024
        ),
        name="constrained",
    )(
        posterior,
        transition,
        emission,
        advance,
        dfa_state.reshape(1, 512),
        edge_next.T,
        token_edge,
        allowed.T,
    )


def solution(mesh):
    in_specs = (
        P(None, "vocab"),
        P("vocab", "hid"),
        P("hid", "vocab"),
        P(None, "hid"),
        P(),
        P(),
        P(None, "vocab"),
        P(None, "vocab"),
    )
    out_specs = P("hid", "vocab")
    return jax.shard_map(body, mesh=mesh, in_specs=in_specs, out_specs=out_specs, check_vma=False)
```

time: 106 us -> 79.4 us (0.75)
  Pallas kernels: 97.5 us -> 77.8 us
  local copies, waits for them, and re-layouts: 8.27 us -> 1.47 us
    pallas_call x1, Pallas kernels: 97.5 us -> 77.8 us  [body(): pl.pallas_call(kernel, out_shape=jax.ShapeDtypeStruct((64, TK), F32), in_...]
    unnamed x17 -> x1, local copies, waits for them, and re-layouts: 8.27 us -> 1.47 us
where the time goes in v2:
time: 79.4 us; the launch traced here: 79.3 us
  Pallas kernels  77.8 us (98%)
  local copies, waits for them, and re-layouts  1.47 us (2%)
    pallas_call x1, Pallas kernels, body(): pl.pallas_call(kernel, out_shape=jax.ShapeDtypeStruct((64, TK), F32), in_...  77.8 us

profile of v2, /device:TPU:1, one launch (start us, length us, event | category | flops | bytes accessed | tf_op | source)
XLA Modules:
  0.0 79.3 jit_solution(5541322626058718113)
XLA Ops:
  0.0 77.8 %constrained.1 = f32[64,256]{1,0:T(8,128)} custom-call(bf16[512,256]{1,0:T(8,128)(2,1)} %post_h.1, bf16[256,2048]{1,0:T(8,128)(2,1)} %trans_h.1, bf16[2048,256]{1,0:T(8,128)(2,1)} %em_h.1, bf16[256,2048]{1,0:T(8,128)(2,1)} %adv_h.1, s32[1,512]{1,0:T(1,128)} %bitcast.5, s32[8,256]{1,0:T(8,128)} %bitcast.3, s32[256,256]{1,0:T(8,128)} %tedge_h.1, s32[2,512]{1,0:T(2,128)} %bitcast.4), custom_call_target="tpu_custom_call" | custom-call | tf_op jit(solution)/shard_map/constrained/pallas_call | solution.py:419
  77.8 1.5 %copy.10 = f32[64,256]{1,0:T(8,128)} copy(f32[64,256]{1,0:T(8,128)} %constrained.1) | data formatting | bytes 131072

commit v3 on v2

--- a/solution.py
+++ b/solution.py
@@ -13,14 +13,15 @@
 HALF = 256
 KC = 1024
 TK = 256
-MW = 384
 TARGET = {
-    -3: 2, -4: 1, -6: -1, -7: -2, 8: -3, 3: -2, 4: -1, 6: 1, 7: 2,
-    1: 1, -1: -1, 2: 2, -2: -2, 5: 5, -5: -5,
+    -4: 1, -6: -1, -7: -2, 8: -3, 4: -1, 6: 1, 7: 2,
+    1: 1, -1: -1, 2: 2, -2: -2, 3: 3, -3: -3, 5: 5, -5: -5,
 }
-FIRST = (8, -3, 3, -7, 7, -4, 4, -6, 6)
-X_ORDER = FIRST + (-5, 5, -2, 2, -1, 1, 0)
-BARRIER_STEPS = (5, -5, 3, -3, 2, -2, 1, -1)
+FIRST = (8, -7, 7, -4, 4, -6, 6)
+X_ORDER = FIRST + (-5, 5, -3, 3, -2, 2, -1, 1, 0)
+BARRIER_STEPS = (3, -3, 2, -2, 1, -1)
+EB = 4
+ER = KC // EB
 
 
 def remote(src, dst, send, recv, a, b):
@@ -70,7 +71,13 @@
     hrecv,
     tsend,
     trecv,
+    usend,
+    urecv,
+    tcol,
+    logs,
     allowed_rows,
+    suc,
+    hot,
     l_in,
     s_c,
     r_c,
@@ -88,6 +95,8 @@
     r_h,
     s_s,
     r_s,
+    s_u,
+    r_u,
 ):
     a = lax.axis_index("vocab")
     b = lax.axis_index("hid")
@@ -101,7 +110,6 @@
     a_x = 4 * z + 2 * oxl + core
 
     half_rows = pl.ds(pl.multiple_of(xl * KC, KC), KC)
-    other_rows = pl.ds(pl.multiple_of(oxl * KC, KC), KC)
     loads = [
         pltpu.make_async_copy(post_h, post, l_in.at[0]),
         pltpu.make_async_copy(trans_h, trans, l_in.at[1]),
@@ -145,6 +153,16 @@
     pl.semaphore_wait(bar, 31 + len(BARRIER_STEPS))
     c0 = remote(csend.at[0], crecv.at[0], s_c.at[0], r_c.at[0], a_core, b)
     c0.start()
+
+    def e_copy(i):
+        rows = pl.ds(pl.multiple_of(oxl * KC + i * ER, ER), ER)
+        return remote(em_h.at[rows, :], em4.at[2, pl.ds(i * ER, ER), :], s_e.at[1 + i], r_e.at[1 + i], a_x, b)
+
+    def f_copy(i):
+        rows = pl.ds(i * ER, ER)
+        return remote(em4.at[2, rows, :], em4.at[3, rows, :], s_e.at[5 + i], r_e.at[5 + i], a_core, b)
+
+    e_copy(0).start()
     csend[1] = part(ocore, xl).astype(BF)
     c1 = remote(csend.at[1], crecv.at[1], s_c.at[1], r_c.at[1], a_core, b)
     c1.start()
@@ -158,10 +176,8 @@
     t_core = remote(tab4.at[0], tab4.at[1], s_t.at[0], r_t.at[0], a_core, b)
     t_x = remote(tab4.at[0], tab4.at[2], s_t.at[1], r_t.at[1], a_x, b)
     t_core.start()
-    t_x.start()
 
     own[0] = part(core, oxl)
-    own[1] = part(core, xl)
     c0.wait_recv()
 
     def x_copy(zc):
@@ -174,49 +190,7 @@
         x_copy(zc).start()
     e_core = remote(em_h.at[half_rows, :], em4.at[1], s_e.at[0], r_e.at[0], a_core, b)
     e_core.start()
-    c1.wait_recv()
-
-    def reduced(o):
-        zc = zmod(z + o)
-        rows = pl.ds(pl.multiple_of(zc * CH, CH), CH)
-        x_copy(zc).wait_recv()
-        return own[1, rows, :] + crecv[1, rows, :].astype(F32) + xrecv[zc].astype(F32)
-
-    def z_copy(o):
-        i = o % NZ
-        return remote(zsend.at[i], zrecv.at[i], s_z.at[i], r_z.at[i], z_dev(TARGET[o]), b)
-
-    def z_send(o, value):
-        zsend[o % NZ] = value.astype(BF)
-        z_copy(o).start()
-
-    def z_take(o):
-        z_copy(o).wait_recv()
-        return zrecv[o % NZ].astype(F32)
-
-    for o in FIRST:
-        z_send(o, reduced(o))
-    agg[0] = reduced(-5)
-    agg[1] = reduced(5)
-    for o in (-2, 2):
-        z_send(o, reduced(o))
-    total = agg[0]
-    for o in (-3, -4, -6, -7, 8):
-        total = total + z_take(o)
-    z_send(-5, total)
-    total = agg[1]
-    for o in (3, 4, 6, 7):
-        total = total + z_take(o)
-    z_send(5, total)
-    for o in (-1, 1):
-        z_send(o, reduced(o))
-    agg[0] = reduced(0)
-
-    e_x = remote(em_h.at[other_rows, :], em4.at[2], s_e.at[1], r_e.at[1], a_x, b)
-    e_x.start()
-    t_x.wait_recv()
-    t_f = remote(tab4.at[2], tab4.at[3], s_t.at[2], r_t.at[2], a_core, b)
-    t_f.start()
+    own[1] = part(core, xl)
 
     for i in (4, 5, 6):
         loads[i].wait()
@@ -225,14 +199,63 @@
     lanes = pl.ds(pl.multiple_of(core * HALF, HALF), HALF)
     hot_t = jnp.where(iota_s == dfa[:, lanes], 1.0, 0.0).astype(F32)
     suc_t = jnp.dot(edge[...].astype(F32).astype(BF), hot_t.astype(BF), preferred_element_type=F32)
-    suc = jnp.transpose(jnp.concatenate([suc_t, jnp.zeros((120, HALF), F32)], axis=0)).astype(jnp.int32)
-    for k in range(8):
-        hot2 = jnp.where(iota_l == suc[:, k : k + 1], 1.0, 0.0).astype(F32).astype(BF)
+    suc[...] = jnp.transpose(jnp.concatenate([suc_t, jnp.zeros((120, HALF), F32)], axis=0)).astype(jnp.int32)
+    hot[...] = jnp.transpose(hot_t).astype(BF)
+
+    def gather(k):
+        hot2 = jnp.where(iota_l == suc[:, pl.ds(k, 1)], 1.0, 0.0).astype(F32).astype(BF)
         g = jnp.dot(hot2, adv[...], preferred_element_type=F32).astype(BF)
         gath[k] = g.reshape(NZ, CH, KC)
 
+    gather(0)
+    gather(1)
+    c1.wait_recv()
+
+    def reduced(o):
+        zc = zmod(z + o)
+        rows = pl.ds(pl.multiple_of(zc * CH, CH), CH)
+        x_copy(zc).wait_recv()
+        return own[1, rows, :] + crecv[1, rows, :].astype(F32) + xrecv[zc].astype(F32)
+
+    def z_copy(o):
+        i = o % NZ
+        return remote(zsend.at[i], zrecv.at[i], s_z.at[i], r_z.at[i], z_dev(TARGET[o]), b)
+
+    def z_send(o, value):
+        zsend[o % NZ] = value.astype(BF)
+        z_copy(o).start()
+
+    def z_take(o):
+        z_copy(o).wait_recv()
+        return zrecv[o % NZ].astype(F32)
+
+    for k, o in enumerate(FIRST):
+        z_send(o, reduced(o))
+        if k < 6:
+            gather(k + 2)
+    low = reduced(-5)
+    for o in (8, -7, -4, -6):
+        low = low + z_take(o)
+    agg[0] = low
+    high = reduced(5)
+    for o in (7, 4, 6):
+        high = high + z_take(o)
+    z_send(-5, agg[0])
+    z_send(5, high)
+    t_x.start()
+    for i in range(1, EB):
+        e_copy(i).start()
+    for o in (-3, 3, -2, 2, -1, 1):
+        z_send(o, reduced(o))
+    agg[0] = reduced(0)
+    e_copy(0).wait_recv()
+    f_copy(0).start()
+    t_x.wait_recv()
+    t_f = remote(tab4.at[2], tab4.at[3], s_t.at[2], r_t.at[2], a_core, b)
+    t_f.start()
+
     total = agg[0]
-    for o in (-1, 1, -2, 2, -5, 5):
+    for o in (-1, 1, -2, 2, -3, 3, -5, 5):
         total = total + z_take(o)
     pri[z] = total.astype(BF)
 
@@ -241,21 +264,21 @@
         i = o % NZ
         return remote(pri.at[zc], pri.at[zc], s_g.at[i], r_g.at[i], z_dev(step), b)
 
-    for step in (5, -5, 1, -1, 2, -2):
+    for step in (5, -5):
         g_copy(0, step, -step).start()
 
-    hot = jnp.transpose(hot_t).astype(BF)
     t_core.wait_recv()
     t_f.wait_recv()
     for j in range(4):
-        te = jnp.dot(hot, tab4[j, pl.ds(0, HALF), :], preferred_element_type=F32)
+        te = jnp.dot(hot[...], tab4[j, pl.ds(0, HALF), :], preferred_element_type=F32)
         al = tab4[j, pl.ds(HALF, 16), :].astype(F32)
         al = jnp.where(core == 0, al[0:2], al[2:4])
         al_t = jnp.transpose(jnp.concatenate([al, jnp.zeros((126, HALF), F32)], axis=0))
         ok = jnp.where(iota_l < 128, al_t[:, 0:1], al_t[:, 1:2])
         te4[j] = jnp.where(ok > 0.0, te, 8.0).astype(BF)
-
-    lane = lax.broadcasted_iota(jnp.int32, (2 * CH, 128), 1)
+    for step in (3, -3, 2, -2, 1, -1):
+        g_copy(0, step, -step).start()
+
     src = xl * 8 + b
 
     def hid_copy(zc, j):
@@ -273,16 +296,16 @@
         remote(pri.at[z], pri.at[zc], s_g.at[i], r_g.at[i], z_dev(1), b).wait_recv()
 
     def score(t, c):
-        m = jnp.where(t < 2, t + 1, jnp.where(t == 2, 5, jnp.where(t == 3, 4, jnp.where(t == 4, 3, t + 1))))
+        m = jnp.where(t == 3, 5, jnp.where(t == 4, 4, t + 1))
         o0 = jnp.where(t == 7, 0, -m)
         zc0 = zmod(z + o0)
         zc1 = zmod(z + m)
 
-        @pl.when(jnp.logical_and(t != 7, t != 2))
+        @pl.when(jnp.logical_and(t != 7, t != 3))
         def _():
             pri_wait(o0)
 
-        @pl.when(t != 2)
+        @pl.when(t != 3)
         def _():
             pri_wait(m)
 
@@ -307,14 +330,11 @@
                 chosen = jnp.where(te == float(k), cand[j, pl.ds(k * 2 * CH, 2 * CH), :], chosen)
             tot = tot + jnp.sum(chosen, axis=1, keepdims=True)
             picked = chosen.astype(BF)
-            hsend[zc0, j, :, pl.ds(0, TK)] = picked[:CH]
-            hsend[zc1, j, :, pl.ds(0, TK)] = picked[CH:]
-        hi = tot.astype(BF).astype(F32)
-        lo = tot - hi
-        tile = jnp.where(lane == 0, hi, jnp.where(lane == 1, lo, 0.0)).astype(BF)
-        for j in range(4):
-            hsend[zc0, j, :, pl.ds(TK, 128)] = tile[:CH]
-            hsend[zc1, j, :, pl.ds(TK, 128)] = tile[CH:]
+            hsend[zc0, j] = picked[:CH]
+            hsend[zc1, j] = picked[CH:]
+        wide = jnp.broadcast_to(tot, (2 * CH, 128))
+        tcol[pl.ds(pl.multiple_of(zc0 * CH, CH), CH), :] = wide[:CH]
+        tcol[pl.ds(pl.multiple_of(zc1 * CH, CH), CH), :] = wide[CH:]
         for zc in (zc0, zc1):
             for j in (3, 2, 1):
                 hid_copy(zc, j).start()
@@ -328,37 +348,28 @@
             def _():
                 hid_copy(zc, 0).start()
 
-        @pl.when(t == 1)
+        @pl.when(t == 0)
         def _():
             pri_wait(-5)
-            for step in (3, -2, 2, -1, 1):
+            for step in (3, 2, -1, 1):
                 g_copy(-5, step, -5 - step).start()
             pri_wait(5)
-            for step in (2, -2, 1, -1):
+            for step in (-2, 1, -1):
                 g_copy(5, step, 5 - step).start()
 
         return c
 
     loads[7].wait()
     e_core.wait_recv()
-    e_x.wait_recv()
-    e_f = remote(em4.at[2], em4.at[3], s_e.at[2], r_e.at[2], a_core, b)
-    e_f.start()
-    e_f.wait_recv()
+    for i in range(1, EB):
+        e_copy(i).wait_recv()
+        f_copy(i).start()
+    for i in range(EB):
+        f_copy(i).wait_recv()
     lax.fori_loop(0, NZ // 2, score, 0)
 
-    def h_wait(i, c):
-        remote(hrecv.at[i], hrecv.at[i], s_h.at[0, 0], r_h.at[i], a_core, b).wait_recv()
-        return c
-
-    lax.fori_loop(0, 16, h_wait, 0)
-    acc = jnp.zeros((64, MW), F32)
-    for i in range(16):
-        acc = acc + hrecv[i].astype(F32)
-    scores = acc[:, :TK]
-    quad_tot = jnp.sum(acc[:, TK:], axis=1, keepdims=True)
-    spread = jnp.concatenate([jnp.broadcast_to(quad_tot, (64, 128)), jnp.zeros((64, 128), F32)], axis=0)
-    tsend[...] = jnp.transpose(spread)[0:1]
+    tsend[0:1] = jnp.transpose(tcol[pl.ds(0, 128), :])[0:1]
+    tsend[1:2] = jnp.transpose(tcol[pl.ds(128, 128), :])[0:1]
 
     def t_copy(i):
         d = zmod(i)
@@ -369,6 +380,16 @@
         return c
 
     lax.fori_loop(0, NZ - 1, t_step, 0)
+    trecv[0] = tsend[...]
+
+    def h_wait(i, c):
+        remote(hrecv.at[i], hrecv.at[i], s_h.at[0, 0], r_h.at[i], a_core, b).wait_recv()
+        return c
+
+    lax.fori_loop(0, 16, h_wait, 0)
+    scores = jnp.zeros((64, TK), F32)
+    for i in range(16):
+        scores = scores + hrecv[i].astype(F32)
     al = tab4[0, pl.ds(HALF, 16), :].astype(F32)
     al = jnp.where(b < 4, al[0:2], al[2:4])
     al_t = jnp.transpose(jnp.concatenate([al, jnp.zeros((126, HALF), F32)], axis=0))
@@ -376,22 +397,53 @@
     al_t = allowed_rows[pl.ds(pl.multiple_of(lax.rem(b, 4) * 64, 64), 64), :]
     lane_v = lax.broadcasted_iota(jnp.int32, (64, TK), 1)
     mask = jnp.where(lane_v < 128, al_t[:, 0:1], al_t[:, 1:2]) > 0.0
-    logs = jnp.log(jnp.where(mask, scores, 1.0))
-    trecv[0] = tsend[...]
+    logs[...] = jnp.log(jnp.where(mask, scores, 1.0))
 
     def t_wait(i, c):
         t_copy(i).wait_recv()
         return c
 
     lax.fori_loop(1, NZ, t_wait, 0)
-    full = jnp.zeros((1, 128), F32)
-    for d in range(NZ):
-        full = full + trecv[d]
-    column = jnp.transpose(jnp.broadcast_to(full, (128, 128)))[:64, 0:1]
-    out[...] = jnp.where(mask, logs - jnp.log(column), 0.0)
-
-    for cp in (c0, c1, e_core, e_x, e_f, t_core, t_x, t_f):
+    part_tot = trecv[0]
+    for d in range(1, NZ):
+        part_tot = part_tot + trecv[d]
+    usend[0] = part_tot[0:1]
+    usend[1] = part_tot[1:2]
+
+    def u_copy(i, j):
+        qa = [q, 2 * xl + ocore, 2 * oxl + core, 2 * oxl + ocore][j]
+        return remote(usend.at[i // 2], urecv.at[src], s_u.at[i, j], r_u.at[src], 4 * z + qa, 4 * core + i)
+
+    for i in range(4):
+        for j in (3, 2, 1):
+            u_copy(i, j).start()
+        mine = 4 * core + i == b
+
+        @pl.when(mine)
+        def _():
+            pltpu.make_async_copy(usend.at[i // 2], urecv.at[src], r_u.at[src]).start()
+
+        @pl.when(jnp.logical_not(mine))
+        def _():
+            u_copy(i, 0).start()
+
+    def u_wait(i, c):
+        remote(urecv.at[i], urecv.at[i], s_u.at[0, 0], r_u.at[i], a_core, b).wait_recv()
+        return c
+
+    lax.fori_loop(0, 16, u_wait, 0)
+    full = urecv[0]
+    for i in range(1, 16):
+        full = full + urecv[i]
+    column = jnp.transpose(jnp.broadcast_to(full, (128, 128)))
+    column = jnp.where(lax.rem(b, 2) == 0, column[:64, 0:1], column[64:, 0:1])
+    out[...] = jnp.where(mask, logs[...] - jnp.log(column), 0.0)
+
+    for cp in (c0, c1, e_core, t_core, t_x, t_f):
         cp.wait_send()
+    for i in range(EB):
+        e_copy(i).wait_send()
+        f_copy(i).wait_send()
 
     def drain(i, c):
         x_copy(i).wait_send()
@@ -411,6 +463,13 @@
         return c
 
     lax.fori_loop(0, NZ, drain, 0)
+    for i in range(4):
+        for j in (1, 2, 3):
+            u_copy(i, j).wait_send()
+
+        @pl.when(4 * core + i != b)
+        def _():
+            u_copy(i, 0).wait_send()
 
 
 def body(posterior, transition, emission, advance, dfa_state, edge_next, token_edge, allowed):
@@ -444,11 +503,17 @@
             pltpu.VMEM((8, NZ, CH, KC), BF),
             pltpu.VMEM((HALF, KC), BF),
             pltpu.VMEM((4, HALF, TK), F32),
-            pltpu.VMEM((NZ, 4, CH, MW), BF),
-            pltpu.VMEM((16, 64, MW), BF),
-            pltpu.VMEM((1, 128), F32),
-            pltpu.VMEM((NZ, 1, 128), F32),
+            pltpu.VMEM((NZ, 4, CH, TK), BF),
+            pltpu.VMEM((16, 64, TK), BF),
+            pltpu.VMEM((2, 128), F32),
+            pltpu.VMEM((NZ, 2, 128), F32),
+            pltpu.VMEM((2, 1, 128), F32),
+            pltpu.VMEM((16, 1, 128), F32),
             pltpu.VMEM((HALF, 128), F32),
+            pltpu.VMEM((64, TK), F32),
+            pltpu.VMEM((HALF, 128), F32),
+            pltpu.VMEM((HALF, 128), jnp.int32),
+            pltpu.VMEM((HALF, HALF), BF),
             dma((8,)),
             dma((2,)),
             dma((2,)),
@@ -458,14 +523,16 @@
             dma((NZ,)),
             dma((NZ,)),
             dma((NZ,)),
-            dma((3,)),
-            dma((3,)),
+            dma((9,)),
+            dma((9,)),
             dma((3,)),
             dma((3,)),
             dma((NZ, 4)),
             dma((16,)),
             dma((NZ,)),
             dma((NZ,)),
+            dma((4, 4)),
+            dma((16,)),
         ],
         compiler_params=pltpu.CompilerParams(
             collective_id=0, has_side_effects=True, vmem_limit_bytes=62 * 1024 * 1024

time: 79.4 us -> 74.5 us (0.938)
  Pallas kernels: 77.8 us -> 72.9 us
    pallas_call x1, Pallas kernels: 77.8 us -> 72.9 us  [body(): pl.pallas_call(kernel, out_shape=jax.ShapeDtypeStruct((64, TK), F32), in_...]
where the time goes in v3:
time: 74.5 us; the launch traced here: 74.3 us
  Pallas kernels  72.9 us (98%)
  local copies, waits for them, and re-layouts  1.47 us (2%)
    pallas_call x1, Pallas kernels, body(): pl.pallas_call(kernel, out_shape=jax.ShapeDtypeStruct((64, TK), F32), in_...  72.9 us

profile of v3, /device:TPU:1, one launch (start us, length us, event | category | flops | bytes accessed | tf_op | source)
XLA Modules:
  0.0 74.3 jit_solution(16149961202929411692)
XLA Ops:
  0.0 72.9 %constrained.1 = f32[64,256]{1,0:T(8,128)} custom-call(bf16[512,256]{1,0:T(8,128)(2,1)} %post_h.1, bf16[256,2048]{1,0:T(8,128)(2,1)} %trans_h.1, bf16[2048,256]{1,0:T(8,128)(2,1)} %em_h.1, bf16[256,2048]{1,0:T(8,128)(2,1)} %adv_h.1, s32[1,512]{1,0:T(1,128)} %bitcast.5, s32[8,256]{1,0:T(8,128)} %bitcast.3, s32[256,256]{1,0:T(8,128)} %tedge_h.1, s32[2,512]{1,0:T(2,128)} %bitcast.4), custom_call_target="tpu_custom_call" | custom-call | tf_op jit(solution)/shard_map/constrained/pallas_call | solution.py:478
  72.9 1.5 %copy.10 = f32[64,256]{1,0:T(8,128)} copy(f32[64,256]{1,0:T(8,128)} %constrained.1) | data formatting | bytes 131072

commit v4 on v3

--- a/solution.py
+++ b/solution.py
@@ -151,8 +151,13 @@
     loads[1].wait()
     csend[0] = part(ocore, oxl).astype(BF)
     pl.semaphore_wait(bar, 31 + len(BARRIER_STEPS))
-    c0 = remote(csend.at[0], crecv.at[0], s_c.at[0], r_c.at[0], a_core, b)
-    c0.start()
+
+    def c_copy(zc):
+        rows = pl.ds(pl.multiple_of(zc * CH, CH), CH)
+        return remote(csend.at[0, rows, :], crecv.at[0, rows, :], s_c.at[zc], r_c.at[zc], a_core, b)
+
+    for o in X_ORDER:
+        c_copy(zmod(z + o)).start()
 
     def e_copy(i):
         rows = pl.ds(pl.multiple_of(oxl * KC + i * ER, ER), ER)
@@ -164,7 +169,7 @@
 
     e_copy(0).start()
     csend[1] = part(ocore, xl).astype(BF)
-    c1 = remote(csend.at[1], crecv.at[1], s_c.at[1], r_c.at[1], a_core, b)
+    c1 = remote(csend.at[1], crecv.at[1], s_c.at[NZ], r_c.at[NZ], a_core, b)
     c1.start()
 
     loads[2].wait()
@@ -178,7 +183,6 @@
     t_core.start()
 
     own[0] = part(core, oxl)
-    c0.wait_recv()
 
     def x_copy(zc):
         return remote(xsend.at[zc], xrecv.at[zc], s_x.at[zc], r_x.at[zc], a_x, b)
@@ -186,6 +190,7 @@
     for o in X_ORDER:
         zc = zmod(z + o)
         rows = pl.ds(pl.multiple_of(zc * CH, CH), CH)
+        c_copy(zc).wait_recv()
         xsend[zc] = (own[0, rows, :] + crecv[0, rows, :].astype(F32)).astype(BF)
         x_copy(zc).start()
     e_core = remote(em_h.at[half_rows, :], em4.at[1], s_e.at[0], r_e.at[0], a_core, b)
@@ -259,13 +264,17 @@
         total = total + z_take(o)
     pri[z] = total.astype(BF)
 
-    def g_copy(chunk, step, o):
-        zc = zmod(z + chunk)
+    def g_copy(chunk, step, o, part_of=None):
+        ref = pri.at[zmod(z + chunk)]
+        if part_of is not None:
+            ref = ref.at[:, pl.ds(part_of * (KC // 2), KC // 2)]
         i = o % NZ
-        return remote(pri.at[zc], pri.at[zc], s_g.at[i], r_g.at[i], z_dev(step), b)
-
-    for step in (5, -5):
-        g_copy(0, step, -step).start()
+        h = part_of or 0
+        return remote(ref, ref, s_g.at[i, h], r_g.at[i, h], z_dev(step), b)
+
+    for h in range(2):
+        for step in (5, -5):
+            g_copy(0, step, -step, h).start()
 
     t_core.wait_recv()
     t_f.wait_recv()
@@ -291,9 +300,12 @@
         return pltpu.make_async_copy(hsend.at[zc, 0], dst, r_h.at[src])
 
     def pri_wait(o):
-        i = zmod(o)
         zc = zmod(z + o)
-        remote(pri.at[z], pri.at[zc], s_g.at[i], r_g.at[i], z_dev(1), b).wait_recv()
+        remote(pri.at[zc], pri.at[zc], s_g.at[zmod(o), 0], r_g.at[zmod(o), 0], z_dev(1), b).wait_recv()
+
+    def pri_wait_half(o, h):
+        ref = pri.at[zmod(z + o), :, pl.ds(h * (KC // 2), KC // 2)]
+        remote(ref, ref, s_g.at[zmod(o), h], r_g.at[zmod(o), h], z_dev(1), b).wait_recv()
 
     def score(t, c):
         m = jnp.where(t == 3, 5, jnp.where(t == 4, 4, t + 1))
@@ -301,13 +313,20 @@
         zc0 = zmod(z + o0)
         zc1 = zmod(z + m)
 
-        @pl.when(jnp.logical_and(t != 7, t != 3))
+        @pl.when(t < 3)
         def _():
             pri_wait(o0)
-
-        @pl.when(t != 3)
-        def _():
             pri_wait(m)
+
+        @pl.when(t > 3)
+        def _():
+            pri_wait_half(m, 0)
+            pri_wait_half(m, 1)
+
+        @pl.when(jnp.logical_and(t > 3, t < 7))
+        def _():
+            pri_wait_half(o0, 0)
+            pri_wait_half(o0, 1)
 
         x0 = pri[zc0]
         x1 = pri[zc1]
@@ -350,12 +369,13 @@
 
         @pl.when(t == 0)
         def _():
-            pri_wait(-5)
-            for step in (3, 2, -1, 1):
-                g_copy(-5, step, -5 - step).start()
-            pri_wait(5)
-            for step in (-2, 1, -1):
-                g_copy(5, step, 5 - step).start()
+            for h in range(2):
+                pri_wait_half(-5, h)
+                for step in (3, 2, -1, 1):
+                    g_copy(-5, step, -5 - step, h).start()
+                pri_wait_half(5, h)
+                for step in (-2, 1, -1):
+                    g_copy(5, step, 5 - step, h).start()
 
         return c
 
@@ -427,6 +447,36 @@
         def _():
             u_copy(i, 0).start()
 
+    for cp in (c1, e_core, t_core, t_x, t_f):
+        cp.wait_send()
+    for i in range(EB):
+        e_copy(i).wait_send()
+        f_copy(i).wait_send()
+
+    def drain(i, c):
+        x_copy(i).wait_send()
+        c_copy(i).wait_send()
+        for j in (1, 2, 3):
+            hid_copy(i, j).wait_send()
+
+        @pl.when(4 * core + i // 4 != b)
+        def _():
+            hid_copy(i, 0).wait_send()
+
+        @pl.when(i > 0)
+        def _():
+            remote(zsend.at[i], zrecv.at[i], s_z.at[i], r_z.at[i], z_dev(1), b).wait_send()
+            t_copy(i).wait_send()
+
+        return c
+
+    lax.fori_loop(0, NZ, drain, 0)
+    for o in (1, 2, 3, -1, -2, -3):
+        g_copy(0, 1, o).wait_send()
+    for o in (4, 5, 6, 7, 8, -4, -5, -6, -7):
+        for h in range(2):
+            g_copy(0, 1, o, h).wait_send()
+
     def u_wait(i, c):
         remote(urecv.at[i], urecv.at[i], s_u.at[0, 0], r_u.at[i], a_core, b).wait_recv()
         return c
@@ -438,31 +488,6 @@
     column = jnp.transpose(jnp.broadcast_to(full, (128, 128)))
     column = jnp.where(lax.rem(b, 2) == 0, column[:64, 0:1], column[64:, 0:1])
     out[...] = jnp.where(mask, logs[...] - jnp.log(column), 0.0)
-
-    for cp in (c0, c1, e_core, t_core, t_x, t_f):
-        cp.wait_send()
-    for i in range(EB):
-        e_copy(i).wait_send()
-        f_copy(i).wait_send()
-
-    def drain(i, c):
-        x_copy(i).wait_send()
-        for j in (1, 2, 3):
-            hid_copy(i, j).wait_send()
-
-        @pl.when(4 * core + i // 4 != b)
-        def _():
-            hid_copy(i, 0).wait_send()
-
-        @pl.when(i > 0)
-        def _():
-            remote(zsend.at[i], zrecv.at[i], s_z.at[i], r_z.at[i], z_dev(1), b).wait_send()
-            remote(pri.at[z], pri.at[z], s_g.at[i], r_g.at[i], z_dev(1), b).wait_send()
-            t_copy(i).wait_send()
-
-        return c
-
-    lax.fori_loop(0, NZ, drain, 0)
     for i in range(4):
         for j in (1, 2, 3):
             u_copy(i, j).wait_send()
@@ -515,14 +540,14 @@
             pltpu.VMEM((HALF, 128), jnp.int32),
             pltpu.VMEM((HALF, HALF), BF),
             dma((8,)),
-            dma((2,)),
-            dma((2,)),
+            dma((NZ + 1,)),
+            dma((NZ + 1,)),
             dma((NZ,)),
             dma((NZ,)),
             dma((NZ,)),
             dma((NZ,)),
-            dma((NZ,)),
-            dma((NZ,)),
+            dma((NZ, 2)),
+            dma((NZ, 2)),
             dma((9,)),
             dma((9,)),
             dma((3,)),

time: 74.5 us -> 74 us (level)
  no operation moved by 1% of the time
where the time goes in v4:
time: 74 us; the launch traced here: 73.8 us
  Pallas kernels  72.3 us (98%)
  local copies, waits for them, and re-layouts  1.47 us (2%)
    pallas_call x1, Pallas kernels, body(): pl.pallas_call(kernel, out_shape=jax.ShapeDtypeStruct((64, TK), F32), in_...  72.3 us

profile of v4, /device:TPU:1, one launch (start us, length us, event | category | flops | bytes accessed | tf_op | source)
XLA Modules:
  0.0 73.8 jit_solution(12570097810112119687)
XLA Ops:
  0.0 72.3 %constrained.1 = f32[64,256]{1,0:T(8,128)} custom-call(bf16[512,256]{1,0:T(8,128)(2,1)} %post_h.1, bf16[256,2048]{1,0:T(8,128)(2,1)} %trans_h.1, bf16[2048,256]{1,0:T(8,128)(2,1)} %em_h.1, bf16[256,2048]{1,0:T(8,128)(2,1)} %adv_h.1, s32[1,512]{1,0:T(1,128)} %bitcast.5, s32[8,256]{1,0:T(8,128)} %bitcast.3, s32[256,256]{1,0:T(8,128)} %tedge_h.1, s32[2,512]{1,0:T(2,128)} %bitcast.4), custom_call_target="tpu_custom_call" | custom-call | tf_op jit(solution)/shard_map/constrained/pallas_call | solution.py:503
  72.4 1.5 %copy.10 = f32[64,256]{1,0:T(8,128)} copy(f32[64,256]{1,0:T(8,128)} %constrained.1) | data formatting | bytes 131072
